TPU v7x, 32 devices: a whole 2x2x4 slice. The times are simulated.
32 devices in a mesh: loop: 4 (over y, x), bulk: 8 (over z, core).
Axes of the slice: x: 2, y: 2, z: 4, core: 2. Of those that a mesh axis runs over, the one named last changes fastest.
Arguments:
- series: float32 [4224, 3072], P('loop', 'bulk'), may hold values from -64 to 64
Outputs:
- correlation: float32 [4, 1056, 4224], P(None, 'bulk', 'loop')
All inputs are finite; a program needn't handle non-finite values.
Results may differ from a plain program's by a relative error of at most 0.0011.
Values may be sent and summed in bfloat16 or wider, within the bound.
A program may use at most 64 MiB of HBM per device.

v0:
```python
import jax
import jax.numpy as jnp
from jax import lax
from jax.sharding import PartitionSpec as P

TIME = 3072
epsilon = 1e-06


def normalize(centered, square_total):
    return (centered * lax.rsqrt(square_total / TIME + epsilon)).astype(jnp.bfloat16)


def contract(first_operand, second_operand):
    product = lax.dot_general(
        first_operand, second_operand, (((1,), (1,)), ((), ())), preferred_element_type=jnp.float32
    )
    return product / TIME


def cycle_gather(own_rows):
    return lax.all_gather(own_rows, "loop", axis=0, tiled=True)


def on_device(series):
    share_rows = series.shape[0] // lax.axis_size("bulk")
    average = lax.psum(jnp.sum(series, axis=1, keepdims=True), "bulk") / TIME
    centered = series - average
    squares = lax.psum(jnp.sum(centered * centered, axis=1, keepdims=True), "bulk")
    zscore = normalize(centered, squares)
    row_series = lax.all_gather(zscore, "bulk", axis=1, tiled=True)
    own_rows = lax.dynamic_slice_in_dim(
        row_series, lax.axis_index("bulk") * share_rows, share_rows, 0
    )
    gathered = contract(cycle_gather(own_rows), row_series)
    return gathered.reshape(lax.axis_size("loop"), share_rows, series.shape[0])


def solution(mesh):
    placed = (P("loop", "bulk"),)
    return jax.shard_map(
        on_device, mesh=mesh, in_specs=placed, out_specs=P(None, "bulk", "loop"), check_vma=False
    )
```

profile of v0, /device:TPU:0, one launch (start us, length us, event | category | flops | bytes accessed | tf_op | source)
XLA Modules:
  0.0 174.9 jit_solution(680406850263193112)
XLA Ops:
  6.5 0.0 copy-start
  6.5 0.0 all-gather.4.cloned.1.call-start
  6.5 1.8 %reduce_sum.18 = f32[1056]{0:T(1024)S(1)} reduce(f32[1056,384]{1,0:T(8,128)} %param.1, f32[]{:T(128)} %constant.7.clone.1), dimensions={1}, to_apply=%region_0.0 | reduce | flops 404448 | bytes 1626244 | tf_op jit(solution)/shard_map/reduce_sum | solution.py:27
  8.3 18.3 %psum.14 = f32[1056,1]{0,1:T(1,128)S(1)} all-reduce(f32[1056,1]{0,1:T(1,128)S(1)} %broadcast_in_dim.6), channel_id=1, replica_groups=mesh['loop'=4,'bulk'=8] {'bulk'}, use_global_device_ids=true, to_apply=%region_1.0 | all-reduce | flops 1056 | bytes 8448 | tf_op jit(solution)/shard_map/psum | solution.py:27
  26.7 0.0 copy-done
  26.7 0.4 multiply_reduce_fusion
  27.1 13.9 %psum.15 = f32[1056,1]{0,1:T(1,128)S(1)} all-reduce(f32[1056,1]{0,1:T(1,128)S(1)} %broadcast_in_dim.7), channel_id=1, replica_groups=mesh['loop'=4,'bulk'=8] {'bulk'}, use_global_device_ids=true, to_apply=%region_3.0 | all-reduce | flops 1056 | bytes 8448 | tf_op jit(solution)/shard_map/psum | solution.py:29
  41.1 1.2 multiply_convert_fusion
  42.3 0.0 all-gather.4.cloned.1.call-update
  42.3 0.0 all-gather.6.cloned.1.call-start
  42.4 64.4 %all-gather.4.cloned.1.call-done = bf16[1056,3072]{1,0:T(8,128)(2,1)} async-done(((bf16[1056,384]{1,0:T(8,128)(2,1)}), bf16[1056,3072]{1,0:T(8,128)(2,1)}) %all-gather.4.cloned.1.call-update) | async-done | bytes 6488080 | tf_op jit(solution)/shard_map/all_gather | solution.py:31
  106.8 2.3 %dynamic-slice_bitcast_fusion = bf16[1,132,3072]{2,1,0:T(8,128)(2,1)} fusion(bf16[1056,3072]{1,0:T(8,128)(2,1)} %all-gather.4.cloned.1.call-done, s32[]{:T(128)S(6)} %select_n.3), kind=kLoop, calls=%fused_computation.3 | loop fusion | bytes 1622020
  109.0 0.0 all-gather.6.cloned.1.call-update
  109.1 44.2 %all-gather.6.cloned.1.call-done = bf16[4,132,3072]{2,1,0:T(8,128)(2,1)} async-done(((bf16[1,132,3072]{2,1,0:T(8,128)(2,1)}), bf16[4,132,3072]{2,1,0:T(8,128)(2,1)}) %all-gather.6.cloned.1.call-update) | async-done | bytes 3244048 | tf_op jit(solution)/shard_map/all_gather | solution.py:22
  153.3 2.3 %reshape.5 = bf16[528,3072]{1,0:T(8,128)(2,1)S(1)} reshape(bf16[4,132,3072]{2,1,0:T(8,128)(2,1)} %all-gather.6.cloned.1.call-done) | data formatting | bytes 6488064
  155.6 8.7 %convolution_multiply_fusion = f32[528,1056]{1,0:T(8,128)} fusion(bf16[528,3072]{1,0:T(8,128)(2,1)S(1)} %reshape.5, bf16[1056,3072]{1,0:T(8,128)(2,1)} %all-gather.4.cloned.1.call-done), kind=kOutput, calls=%fused_computation | convolution fusion | flops 3426255360 | bytes 11962368 | tf_op jit(solution)/shard_map/dot_general | solution.py:15
  164.2 1.8 %reshape.3 = f32[4,132,1056]{2,1,0:T(8,128)S(1)} reshape(f32[528,1056]{1,0:T(8,128)} %convolution_multiply_fusion) | data formatting | bytes 4460544 | tf_op jit(solution)/shard_map/reshape | solution.py:36
  166.0 2.1 %copy.4 = f32[4,132,1056]{2,0,1:T(4,128)} copy(f32[4,132,1056]{2,1,0:T(8,128)S(1)} %reshape.3) | data formatting | bytes 4460544 | tf_op jit(solution)/shard_map/reshape | solution.py:36
  (4 shorter events, 0.1 us)
Async XLA Ops:
  6.5 20.2 %copy-start = (f32[1056,384]{1,0:T(8,128)S(1)}, f32[1056,384]{1,0:T(8,128)}, u32[]{:S(2)}) copy-start(f32[1056,384]{1,0:T(8,128)} %param.1) | copy-start | bytes 4866052
  6.5 100.2 %all-gather.4.cloned.1.call-start = ((), (), s32[]{:S(2)}) async-start(), calls=%async_computation | async-start | bytes 7299072 | tf_op jit(solution)/shard_map/all_gather | solution.py:31
  42.3 110.9 %all-gather.6.cloned.1.call-start = ((), (), s32[]{:S(2)}) async-start(), calls=%async_computation.1 | async-start | bytes 4177920 | tf_op jit(solution)/shard_map/all_gather | solution.py:22
Sparse Core Ops, SparseCore 0:
  42.5 64.2 all-gather.3
  109.2 44.0 all-gather.5
where the time goes:
time: 175 us
  waiting for transfers between devices  109 us (62%)
  blocking collectives  32.3 us (18%)
  between operations  13.5 us (8%)
  matrix products  8.65 us (5%)
  local copies, waits for them, and re-layouts  8.41 us (5%)
  other arithmetic  3.46 us (2%)
    all_gather x1, waiting for transfers between devices, on_device(): row_series = lax.all_gather(zscore, 'bulk', axis=1, tiled=True)  64.4 us
    all_gather x1, waiting for transfers between devices, cycle_gather(): return lax.all_gather(own_rows, 'loop', axis=0, tiled=True)  44.2 us
    psum x1, blocking collectives, on_device(): average = lax.psum(jnp.sum(series, axis=1, keepdims=True), 'bulk') / TIME  18.3 us
    psum x1, blocking collectives, on_device(): lax.psum(jnp.sum(centered * centered, axis=1, keepdims=True), 'bulk')  13.9 us
    dot_general x1, matrix products, contract(): lax.dot_general(first_operand, second_operand, (((1,), (1,)), ((), ())),...  8.65 us
    unnamed x4, local copies, waits for them, and re-layouts  4.55 us
    reshape x2, local copies, waits for them, and re-layouts, on_device(): return gathered.reshape(lax.axis_size('loop'), share_rows, series.shape[0])  3.84 us
  transfers between devices with their start and end apart: 2, of which 2 were waited for; matrix products, arithmetic and copies ran while one was open for 0% of the time, Pallas kernels for 0%

commit v1 on v0

--- a/solution.py
+++ b/solution.py
@@ -26,7 +26,9 @@
     share_rows = series.shape[0] // lax.axis_size("bulk")
     average = lax.psum(jnp.sum(series, axis=1, keepdims=True), "bulk") / TIME
     centered = series - average
-    squares = lax.psum(jnp.sum(centered * centered, axis=1, keepdims=True), "bulk")
+    x = jnp.sum(centered * centered, axis=1, keepdims=True)
+    pieces = lax.all_gather(x, "bulk", axis=0, tiled=False)
+    squares = pieces.sum(axis=0)
     zscore = normalize(centered, squares)
     row_series = lax.all_gather(zscore, "bulk", axis=1, tiled=True)
     own_rows = lax.dynamic_slice_in_dim(

time: 175 us -> 189 us (1.080)
  blocking collectives: 32.3 us -> 44.6 us
    unnamed x0 -> x1, blocking collectives: none -> 26.3 us
    psum x1 -> x0, blocking collectives: 13.9 us -> none  [on_device(): lax.psum(jnp.sum(centered * centered, axis=1, keepdims=True), 'bulk')]
    unnamed x4 -> x9, local copies, waits for them, and re-layouts: 4.55 us -> 5.47 us
where the time goes in v1:
time: 189 us
  waiting for transfers between devices  109 us (58%)
  blocking collectives  44.6 us (24%)
  between operations  14.1 us (7%)
  local copies, waits for them, and re-layouts  9.41 us (5%)
  matrix products  8.66 us (5%)
  other arithmetic  3.47 us (2%)
    all_gather x1, waiting for transfers between devices, on_device(): row_series = lax.all_gather(zscore, 'bulk', axis=1, tiled=True)  64.4 us
    all_gather x1, waiting for transfers between devices, cycle_gather(): return lax.all_gather(own_rows, 'loop', axis=0, tiled=True)  44.2 us
    unnamed x1, blocking collectives  26.3 us
    psum x1, blocking collectives, on_device(): average = lax.psum(jnp.sum(series, axis=1, keepdims=True), 'bulk') / TIME  18.3 us
    dot_general x1, matrix products, contract(): lax.dot_general(first_operand, second_operand, (((1,), (1,)), ((), ())),...  8.66 us
    unnamed x9, local copies, waits for them, and re-layouts  5.47 us
    reshape x2, local copies, waits for them, and re-layouts, on_device(): return gathered.reshape(lax.axis_size('loop'), share_rows, series.shape[0])  3.84 us
  transfers between devices with their start and end apart: 2, of which 2 were waited for; matrix products, arithmetic and copies ran while one was open for 0% of the time, Pallas kernels for 0%

profile of v1, /device:TPU:0, one launch (start us, length us, event | category | flops | bytes accessed | tf_op | source)
XLA Modules:
  0.0 189.0 jit_solution(8914373802729485387)
XLA Ops:
  6.5 0.0 copy-start.1
  6.5 0.0 copy-start
  6.5 0.0 all-gather.5.cloned.1.call-start
  6.5 1.8 reduce_sum.27
  8.3 18.3 %psum.7 = f32[1056,1]{0,1:T(1,128)S(1)} all-reduce(f32[1056,1]{0,1:T(1,128)S(1)} %broadcast_in_dim.3), channel_id=1, replica_groups=mesh['loop'=4,'bulk'=8] {'bulk'}, use_global_device_ids=true, to_apply=%region_1.0 | all-reduce | flops 1056 | bytes 8448 | tf_op jit(solution)/shard_map/psum | solution.py:27
  26.7 0.0 copy-done
  26.7 0.4 multiply_reduce_fusion
  27.1 0.0 copy-done.1
  27.1 0.6 dynamic-slice
  28.4 0.3 dynamic-update-slice
  28.7 26.3 %all-reduce = f32[8448]{0:T(1024)S(1)} all-reduce(f32[8448]{0:T(1024)S(1)} %dynamic-update-slice), channel_id=2, replica_groups=mesh['loop'=4,'bulk'=8] {'bulk'}, use_global_device_ids=true, to_apply=%add | all-reduce | flops 8448 | bytes 67584
  55.0 0.1 reshape.13
  55.1 1.2 multiply_convert_fusion
  56.4 0.0 all-gather.5.cloned.1.call-update
  56.4 0.0 all-gather.7.cloned.1.call-start
  56.4 64.4 %all-gather.5.cloned.1.call-done = bf16[1056,3072]{1,0:T(8,128)(2,1)} async-done(((bf16[1056,384]{1,0:T(8,128)(2,1)}), bf16[1056,3072]{1,0:T(8,128)(2,1)}) %all-gather.5.cloned.1.call-update) | async-done | bytes 6488080 | tf_op jit(solution)/shard_map/all_gather | solution.py:33
  120.8 2.3 %dynamic-slice_bitcast_fusion = bf16[1,132,3072]{2,1,0:T(8,128)(2,1)} fusion(bf16[1056,3072]{1,0:T(8,128)(2,1)} %all-gather.5.cloned.1.call-done, s32[]{:T(128)S(6)} %select_n.3), kind=kLoop, calls=%fused_computation.3 | loop fusion | bytes 1622020
  123.1 0.0 all-gather.7.cloned.1.call-update
  123.1 44.2 %all-gather.7.cloned.1.call-done = bf16[4,132,3072]{2,1,0:T(8,128)(2,1)} async-done(((bf16[1,132,3072]{2,1,0:T(8,128)(2,1)}), bf16[4,132,3072]{2,1,0:T(8,128)(2,1)}) %all-gather.7.cloned.1.call-update) | async-done | bytes 3244048 | tf_op jit(solution)/shard_map/all_gather | solution.py:22
  167.3 2.3 %reshape.19 = bf16[528,3072]{1,0:T(8,128)(2,1)S(1)} reshape(bf16[4,132,3072]{2,1,0:T(8,128)(2,1)} %all-gather.7.cloned.1.call-done) | data formatting | bytes 6488064
  169.6 8.7 %convolution_multiply_fusion = f32[528,1056]{1,0:T(8,128)} fusion(bf16[528,3072]{1,0:T(8,128)(2,1)S(1)} %reshape.19, bf16[1056,3072]{1,0:T(8,128)(2,1)} %all-gather.5.cloned.1.call-done), kind=kOutput, calls=%fused_computation | convolution fusion | flops 3426255360 | bytes 11962368 | tf_op jit(solution)/shard_map/dot_general | solution.py:15
  178.3 1.8 reshape.12
  180.1 2.1 %copy.5 = f32[4,132,1056]{2,0,1:T(4,128)} copy(f32[4,132,1056]{2,1,0:T(8,128)S(1)} %reshape.12) | data formatting | bytes 4460544 | tf_op jit(solution)/shard_map/reshape | solution.py:38
  (5 shorter events, 0.1 us)
Async XLA Ops:
  6.5 20.6 %copy-start.1 = (u32[32]{0:T(128)S(1)}, u32[32]{0:T(128)}, u32[]{:S(2)}) copy-start(u32[32]{0:T(128)} %constant.22) | copy-start | bytes 388
  6.5 20.2 %copy-start = (f32[1056,384]{1,0:T(8,128)S(1)}, f32[1056,384]{1,0:T(8,128)}, u32[]{:S(2)}) copy-start(f32[1056,384]{1,0:T(8,128)} %param.1) | copy-start | bytes 4866052
  6.5 114.3 %all-gather.5.cloned.1.call-start = ((), (), s32[]{:S(2)}) async-start(), calls=%async_computation | async-start | bytes 7299072 | tf_op jit(solution)/shard_map/all_gather | solution.py:33
  56.4 110.9 %all-gather.7.cloned.1.call-start = ((), (), s32[]{:S(2)}) async-start(), calls=%async_computation.1 | async-start | bytes 4177920 | tf_op jit(solution)/shard_map/all_gather | solution.py:22
Sparse Core Ops, SparseCore 0:
  56.5 64.2 all-gather.4
  123.2 44.0 all-gather.6
